TPU v7x, 128 devices: a whole 4x4x4 slice. The times are simulated.
128 devices in a mesh: region: 16 (over y_lo, z, core), group: 8 (over y_hi, x).
Axes of the slice: x: 4, y: 4 (y_hi: 2, y_lo: 2; y = y_hi * 2 + y_lo), z: 4, core: 2. Of those that a mesh axis runs over, the one named last changes fastest.
Arguments:
- object_slab: float32 [8192, 2, 4096], P('region', None, 'group'), may hold values from -6 to 6
- probe: float32 [4, 2, 256, 256], replicated, may hold values from -6 to 6
- diffraction: float32 [512, 256, 256], P(('region', 'group')), may hold values from 0.25 to 16
- positions: int32 [512, 2], P(('region', 'group')), may hold values from 0 to 7936, as said below
- slot_counts: int32 [8, 16], P('group', 'region'), may hold values from 1 to 4, 40 in all within a row
Outputs:
- new_object: float32 [8192, 2, 4096], P('region', None, 'group')
- new_probe: float32 [4, 2, 256, 256], replicated
Inputs may be any that keep to these rules, and one draw needn't show every extreme that they name: `positions`: A slot of region index r has its row in r * 512 to min(r * 512 + 511, 7936); columns lie in 0 to 256; rows 0 and 7936 and columns 0 and 256 are each taken by some slot.
All inputs are finite; a program needn't handle non-finite values. No bound on the sum of `slot_counts` on one device may be relied on, other than what follows from the above.
Results may differ from a plain program's by a relative error of at most 0.0003.
Values sent between devices are 32-bit elements; how exact they have to be, the bound alone decides.
A program may use at most 128 MiB of HBM per device.

v0:
```python
import math
import jax
import jax.numpy as jnp
from jax import lax
from jax.sharding import PartitionSpec as P

highest = lax.Precision.HIGHEST


def shifted(block, axis, distance):
    devices = range(lax.axis_size(axis))
    route = [(i - distance, i) for i in devices if i - distance in devices]
    return lax.ppermute(block, axis, route)


def tables(side):
    index = jnp.arange(side, dtype=jnp.int32)
    prod = index[:, None] * index[None, :] % side
    angle = prod.astype(jnp.float32) * (2.0 * math.pi / side)
    scale = 1.0 / math.sqrt(side)
    return (jnp.cos(angle) * scale, -jnp.sin(angle) * scale)


def transform(real_part, imag_part, cos_tab, sin_tab):
    left_r = jnp.einsum("jk,mkl->mjl", cos_tab, real_part, precision=highest) - jnp.einsum(
        "jk,mkl->mjl", sin_tab, imag_part, precision=highest
    )
    left_i = jnp.einsum("jk,mkl->mjl", cos_tab, imag_part, precision=highest) + jnp.einsum(
        "jk,mkl->mjl", sin_tab, real_part, precision=highest
    )
    out_r = jnp.einsum("mjk,kl->mjl", left_r, cos_tab, precision=highest) - jnp.einsum(
        "mjk,kl->mjl", left_i, sin_tab, precision=highest
    )
    out_i = jnp.einsum("mjk,kl->mjl", left_r, sin_tab, precision=highest) + jnp.einsum(
        "mjk,kl->mjl", left_i, cos_tab, precision=highest
    )
    return (out_r, out_i)


def on_device(object_slab, probe, diffraction, positions, slot_counts):
    side = probe.shape[2]
    slots = diffraction.shape[0]
    tile_rows = object_slab.shape[0]
    active_count = slot_counts[0, 0]
    cos_tab, sin_tab = tables(side)
    base = lax.axis_index("region") * tile_rows
    local_rows = positions[:, 0] - base
    shard_columns = positions[:, 1]
    obj = object_slab
    prb = probe
    peak = jnp.max(jnp.sum(prb[:, 0] * prb[:, 0] + prb[:, 1] * prb[:, 1], axis=0))
    below = shifted(obj, "region", -1)
    extended = jnp.concatenate([obj, below], axis=0)

    def cut(row, col):
        return lax.dynamic_slice(extended, (row, jnp.int32(0), col), (side, 2, side))

    windows = jax.vmap(cut)(local_rows, shard_columns)
    probe_r = prb[:, 0]
    probe_i = prb[:, 1]

    def single_position(position_entry, carry):
        wgrads, pgrad, cover = carry
        live = (position_entry < active_count).astype(jnp.float32)
        win = lax.dynamic_index_in_dim(windows, position_entry, 0, keepdims=False)
        observed_intensity = lax.dynamic_index_in_dim(
            diffraction, position_entry, 0, keepdims=False
        )
        win_r = win[:, 0, :]
        win_i = win[:, 1, :]
        exit_r = probe_r * win_r[None] - probe_i * win_i[None]
        exit_i = probe_r * win_i[None] + probe_i * win_r[None]
        far_r, far_i = transform(exit_r, exit_i, cos_tab, sin_tab)
        model_intensity = jnp.sum(far_r * far_r + far_i * far_i, axis=0)
        update_ratio = 1.0 - jnp.sqrt(observed_intensity) / jnp.sqrt(
            jnp.maximum(model_intensity, 1.0)
        )
        chi_r, chi_i = transform(
            far_r * update_ratio[None], far_i * update_ratio[None], cos_tab, -sin_tab
        )
        chi_r = chi_r * live
        chi_i = chi_i * live
        go_r = jnp.sum(probe_r * chi_r + probe_i * chi_i, axis=0)
        go_i = jnp.sum(probe_r * chi_i - probe_i * chi_r, axis=0)
        grad_win = jnp.stack([go_r, go_i], axis=1)
        wgrads = lax.dynamic_update_index_in_dim(wgrads, grad_win, position_entry, 0)
        gp = jnp.stack(
            [win_r[None] * chi_r + win_i[None] * chi_i, win_r[None] * chi_i - win_i[None] * chi_r],
            axis=1,
        )
        return (wgrads, pgrad + gp, cover + live * (win_r * win_r + win_i * win_i))

    start_carry = (
        jnp.zeros((slots, side, 2, side), jnp.float32),
        jnp.zeros(prb.shape, jnp.float32),
        jnp.zeros((side, side), jnp.float32),
    )
    wgrads, pgrad, cover = lax.fori_loop(0, slots, single_position, start_carry)
    pgrad, cover = lax.psum((pgrad, cover), ("region", "group"))

    def put(position_entry, scratch_array):
        row = local_rows[position_entry]
        col = shard_columns[position_entry]
        current = lax.dynamic_slice(scratch_array, (row, jnp.int32(0), col), (side, 2, side))
        return lax.dynamic_update_slice(
            scratch_array, current + wgrads[position_entry], (row, jnp.int32(0), col)
        )

    scratch_array = lax.fori_loop(0, slots, put, jnp.zeros(extended.shape, jnp.float32))
    tile_grad = scratch_array[:tile_rows]
    spill = scratch_array[tile_rows:]
    arrived = shifted(spill, "region", 1)
    tile_grad = tile_grad + arrived
    obj = obj - tile_grad / peak
    prb = prb - pgrad / (cover + 1e-06)[None, None]
    return (obj, prb)


def solution(mesh):
    placed = (
        P("region", None, "group"),
        P(),
        P(("region", "group"), None, None),
        P(("region", "group"), None),
        P("group", "region"),
    )
    return jax.shard_map(
        on_device,
        mesh=mesh,
        in_specs=placed,
        out_specs=(P("region", None, "group"), P()),
        check_vma=False,
    )
```

profile of v0, /device:TPU:1, one launch (start us, length us, event | category | flops | bytes accessed | tf_op | source)
XLA Modules:
  0.0 704.6 jit_solution(1375702932699397892)
XLA Ops:
  13.6 22.5 %collective-permute-done = f32[512,2,512]{2,1,0:T(2,128)} collective-permute-done((f32[512,2,512]{2,1,0:T(2,128)}, f32[512,2,512]{2,1,0:T(2,128)}, u32[]{:S(2)}, u32[]{:S(2)}) %collective-permute-start) | collective-permute-done | bytes 2097184 | tf_op jit(solution)/shard_map/ppermute | solution.py:13
  36.2 5.3 pad_maximum_fusion
  43.4 17.1 %while.35 = (s32[]{:T(128)}, f32[1024,2,512]{2,1,0:T(2,128)}, s32[4,3]{1,0:T(4,128)S(1)}, f32[4,256,2,256]{3,2,1,0:T(2,128)}, s32[]{:T(128)}) while((s32[]{:T(128)}, f32[1024,2,512]{2,1,0:T(2,128)}, s32[4,3]{1,0:T(4,128)S(1)}, f32[4,256,2,256]{3,2,1,0:T(2,128)}, s32[]{:T(128)}) %tuple.99), condition=%wide.while_cond, body=%wide.while_body.sunk | while | flops 2 | bytes 1050217 | solution.py:56
  43.9 3.7 bitcast_dynamic-update-slice_fusion.2
  48.2 3.7 bitcast_dynamic-update-slice_fusion.2
  52.5 3.7 bitcast_dynamic-update-slice_fusion.2
  56.8 3.7 bitcast_dynamic-update-slice_fusion.2
  62.3 249.9 %while.36 = (s32[]{:T(128)}, f32[4,256,2,256]{3,2,1,0:T(2,128)}, f32[4,2,256,256]{3,2,0,1:T(8,128)}, f32[256,256]{1,0:T(8,128)}, f32[4,256,2,256]{3,2,1,0:T(2,12...) while((s32[]{:T(128)}, f32[4,256,2,256]{3,2,1,0:T(2,128)}, ...), condition=%wide.region_4.5_spmd.clone.clone, body=%wide.region_0.4_spmd.clone.clone.sunk | while | flops 12915048448 | bytes 82838280 | solution.py:98
  100.1 3.7 fusion.229
  104.4 4.6 fusion.232
  111.7 5.4 add_bitcast_fusion.2
  160.1 3.7 fusion.229
  164.5 4.8 fusion.232
  172.0 5.4 add_bitcast_fusion.2
  177.3 3.9 maximum_add_fusion.2
  212.0 3.7 fusion.231
  222.1 3.7 fusion.229
  226.4 4.5 fusion.232
  233.6 5.4 add_bitcast_fusion.2
  239.0 3.9 maximum_add_fusion.2
  283.7 3.7 fusion.229
  288.1 4.6 fusion.232
  295.3 5.4 add_bitcast_fusion.2
  300.7 3.9 maximum_add_fusion.2
  315.3 207.1 %while.34 = (s32[]{:T(128)}, f32[1024,2,512]{2,1,0:T(2,128)}, s32[4]{0:T(128)S(1)}, s32[4]{0:T(128)S(1)}, f32[4,256,2,256]{3,2,1,0:T(2,128)}, /*index=5*/s32[]{:T(128)}, s32[]{:T(128)}, s32[]{:T(128)}, s32[]{:T(128)}) while((s32[]{:T(128)}, f32[1024,2,512]{2,1,0:T(2,128)}, s32[4]{0:T(128)S(1)}, s32[4]{0:T(128)S(1)}, ...), condition=%wide.region_6.7_spmd, body=%wide.region_5.6_spmd.sunk | while | flops 131080 | bytes 2621641 | solution.py:109
  322.1 45.0 %dynamic_update_slice.21 = f32[1024,2,512]{2,1,0:T(2,128)} dynamic-update-slice(f32[1024,2,512]{2,1,0:T(2,128)} %get-tuple-element.735, f32[256,2,256]{2,1,0:T(2,128)S(1)} %bitcast_add_fusion.2, s32[]{:T(128)S(6)} %select_n.175, s32[]{:T(128)} %constant.116.clone.1..sunk, s32[]{:T(128)S(6)} %select_n.176) | dynamic-update-slice | bytes 1048580 | tf_op jit(solution)/shard_map/while/body/eval_jaxpr/dynamic_update_slice | solution.py:105
  373.8 45.0 %dynamic_update_slice.21 = f32[1024,2,512]{2,1,0:T(2,128)} dynamic-update-slice(f32[1024,2,512]{2,1,0:T(2,128)} %get-tuple-element.735, f32[256,2,256]{2,1,0:T(2,128)S(1)} %bitcast_add_fusion.2, s32[]{:T(128)S(6)} %select_n.175, s32[]{:T(128)} %constant.116.clone.1..sunk, s32[]{:T(128)S(6)} %select_n.176) | dynamic-update-slice | bytes 1048580 | tf_op jit(solution)/shard_map/while/body/eval_jaxpr/dynamic_update_slice | solution.py:105
  425.6 45.0 %dynamic_update_slice.21 = f32[1024,2,512]{2,1,0:T(2,128)} dynamic-update-slice(f32[1024,2,512]{2,1,0:T(2,128)} %get-tuple-element.735, f32[256,2,256]{2,1,0:T(2,128)S(1)} %bitcast_add_fusion.2, s32[]{:T(128)S(6)} %select_n.175, s32[]{:T(128)} %constant.116.clone.1..sunk, s32[]{:T(128)S(6)} %select_n.176) | dynamic-update-slice | bytes 1048580 | tf_op jit(solution)/shard_map/while/body/eval_jaxpr/dynamic_update_slice | solution.py:105
  477.4 45.0 %dynamic_update_slice.21 = f32[1024,2,512]{2,1,0:T(2,128)} dynamic-update-slice(f32[1024,2,512]{2,1,0:T(2,128)} %get-tuple-element.735, f32[256,2,256]{2,1,0:T(2,128)S(1)} %bitcast_add_fusion.2, s32[]{:T(128)S(6)} %select_n.175, s32[]{:T(128)} %constant.116.clone.1..sunk, s32[]{:T(128)S(6)} %select_n.176) | dynamic-update-slice | bytes 1048580 | tf_op jit(solution)/shard_map/while/body/eval_jaxpr/dynamic_update_slice | solution.py:105
  522.3 3.8 slice.43
  532.0 155.4 %all-reduce.3.cloned.1.call-done = (f32[4,2,256,256]{3,2,1,0:T(8,128)}, f32[256,256]{1,0:T(8,128)}) async-done(((f32[4,2,256,256]{3,2,1,0:T(8,128)}, f32[256,256]{1,0:T(8,128)}), (f32[4,2,256,256]{3,2,1,0:T(8,128)}, f32[256,256]{1,0:T(8,128)})) %all-reduce.3.cloned.1.call-update) | async-done | bytes 2359312 | tf_op jit(solution)/shard_map/psum | solution.py:99
  692.7 4.9 divide_subtract_fusion
  (169 shorter events, 210.5 us)
Async XLA Ops:
  7.2 680.3 %all-reduce.3.cloned.1.call-start = ((), (), s32[]{:S(2)}) async-start(), calls=%async_computation | async-start | bytes 4718592 | tf_op jit(solution)/shard_map/psum | solution.py:99
  7.2 29.0 %collective-permute-start = (f32[512,2,512]{2,1,0:T(2,128)}, f32[512,2,512]{2,1,0:T(2,128)}, u32[]{:S(2)}, u32[]{:S(2)}) collective-permute-start(f32[512,2,512]{2,1,0:T(2,128)} %param.9), channel_id=1, source_target_pairs={{8,0},{16,8},{24,16},{32,24},{40,32},{48,40},{56,48},{64,56},{72,6... | collective-permute-start | bytes 6291464 | tf_op jit(solution)/shard_map/ppermute | solution.py:13
  11.7 24.5 %copy-start.7 = (f32[512,2,512]{2,1,0:T(2,128)S(1)}, f32[512,2,512]{2,1,0:T(2,128)}, u32[]{:S(2)}) copy-start(f32[512,2,512]{2,1,0:T(2,128)} %param.9) | copy-start | bytes 6291460
  99.0 1.0 copy-start.1
  104.4 4.6 copy-start.2
  104.4 7.3 %copy-start = (f32[4,256,256]{1,2,0:T(8,128)S(1)}, f32[4,256,256]{1,2,0:T(8,128)}, u32[]{:S(2)}) copy-start(f32[4,256,256]{1,2,0:T(8,128)} %fusion.231) | copy-start | bytes 3145732 | tf_op jit(solution)/shard_map/while
  117.0 3.2 copy-start.5
  159.1 1.0 copy-start.1
  164.5 4.8 copy-start.2
  164.5 7.5 %copy-start = (f32[4,256,256]{1,2,0:T(8,128)S(1)}, f32[4,256,256]{1,2,0:T(8,128)}, u32[]{:S(2)}) copy-start(f32[4,256,256]{1,2,0:T(8,128)} %fusion.231) | copy-start | bytes 3145732 | tf_op jit(solution)/shard_map/while
  177.3 3.9 copy-start.5
  221.0 1.0 copy-start.1
  226.4 4.6 copy-start.2
  226.4 7.2 %copy-start = (f32[4,256,256]{1,2,0:T(8,128)S(1)}, f32[4,256,256]{1,2,0:T(8,128)}, u32[]{:S(2)}) copy-start(f32[4,256,256]{1,2,0:T(8,128)} %fusion.231) | copy-start | bytes 3145732 | tf_op jit(solution)/shard_map/while
  239.0 3.9 copy-start.5
  282.7 1.0 copy-start.1
  288.0 4.6 copy-start.2
  288.1 7.3 %copy-start = (f32[4,256,256]{1,2,0:T(8,128)S(1)}, f32[4,256,256]{1,2,0:T(8,128)}, u32[]{:S(2)}) copy-start(f32[4,256,256]{1,2,0:T(8,128)} %fusion.231) | copy-start | bytes 3145732 | tf_op jit(solution)/shard_map/while
  300.7 3.9 copy-start.5
  522.3 5.7 copy-start.3
  526.2 165.7 %collective-permute-start.1 = (f32[512,2,512]{2,1,0:T(2,128)}, f32[512,2,512]{2,1,0:T(2,128)}, u32[]{:S(2)}, u32[]{:S(2)}) collective-permute-start(f32[512,2,512]{2,1,0:T(2,128)} %slice.43), channel_id=1, source_target_pairs={{0,8},{8,16},{16,24},{24,32},{32,40},{40,48},{48,56},{56,64},{64,7... | collective-permute-start | bytes 6291464 | tf_op jit(solution)/shard_map/ppermute | solution.py:13
  529.6 1.6 copy-start.6
  688.4 3.4 copy-start.4
  688.4 4.2 copy-start.8
Sparse Core Ops, SparseCore 0:
  529.8 157.6 all-reduce.2
where the time goes:
time: 710 us; the launch traced here: 705 us
  local copies, waits for them, and re-layouts  230 us (32%)
  matrix products  201 us (28%)
  waiting for transfers between devices  178 us (25%)
  other arithmetic  53.2 us (7%)
  loops' own time  23.3 us (3%)
  between operations  14.3 us (2%)
    dynamic_update_slice x4, local copies, waits for them, and re-layouts, put(): lax.dynamic_update_slice(scratch_array, current + wgrads[position_entry],...  180 us
    psum x1, waiting for transfers between devices, on_device(): pgrad, cover = lax.psum((pgrad, cover), ('region', 'group'))  155 us
    dot_general x8, matrix products, transform(): jnp.einsum('mjk,kl->mjl', left_i, sin_tab, precision=highest)  32.1 us
    dot_general x8, matrix products, transform(): jnp.einsum('mjk,kl->mjl', left_i, cos_tab, precision=highest)  29.2 us
    dot_general x8, matrix products, transform(): jnp.einsum('jk,mkl->mjl', sin_tab, real_part, precision=highest)  25.5 us
    dot_general x8, matrix products, transform(): jnp.einsum('mjk,kl->mjl', left_r, sin_tab, precision=highest)  25.3 us
    dot_general x8, matrix products, transform(): jnp.einsum('mjk,kl->mjl', left_r, cos_tab, precision=highest)  22.6 us
    ppermute x2, waiting for transfers between devices, shifted(): return lax.ppermute(block, axis, route)  22.5 us
  transfers between devices with their start and end apart: 3, of which 2 were waited for; matrix products, arithmetic and copies ran while one was open for 1% of the time, Pallas kernels for 0%

commit v1 on v0

--- a/solution.py
+++ b/solution.py
@@ -96,7 +96,7 @@
         jnp.zeros((side, side), jnp.float32),
     )
     wgrads, pgrad, cover = lax.fori_loop(0, slots, single_position, start_carry)
-    pgrad, cover = lax.psum((pgrad, cover), ("region", "group"))
+    pgrad, cover = lax.psum(lax.psum((pgrad, cover), "region"), "group")
 
     def put(position_entry, scratch_array):
         row = local_rows[position_entry]

time: 710 us -> 649 us (0.914)
  waiting for transfers between devices: 178 us -> 111 us
    psum x1 -> x2, waiting for transfers between devices: 155 us -> 65.9 us  [on_device(): pgrad, cover = lax.psum(lax.psum((pgrad, cover), 'region'), 'group')]
    ppermute x2, waiting for transfers between devices: 22.5 us -> 44.9 us  [shifted(): return lax.ppermute(block, axis, route)]
  transfers between devices with their start and end apart: 3 -> 4, of which waited for: 2 -> 3; matrix products, arithmetic and copies ran while one was open for 1% -> 33% of each run, Pallas kernels for 0% -> 0%
where the time goes in v1:
time: 649 us; the launch traced here: 639 us
  local copies, waits for them, and re-layouts  230 us (35%)
  matrix products  200 us (31%)
  waiting for transfers between devices  111 us (17%)
  other arithmetic  53.3 us (8%)
  loops' own time  25 us (4%)
  between operations  14.3 us (2%)
    dynamic_update_slice x4, local copies, waits for them, and re-layouts, put(): lax.dynamic_update_slice(scratch_array, current + wgrads[position_entry],...  180 us
    psum x2, waiting for transfers between devices, on_device(): pgrad, cover = lax.psum(lax.psum((pgrad, cover), 'region'), 'group')  65.9 us
    ppermute x2, waiting for transfers between devices, shifted(): return lax.ppermute(block, axis, route)  44.9 us
    dot_general x8, matrix products, transform(): jnp.einsum('mjk,kl->mjl', left_i, sin_tab, precision=highest)  32.1 us
    dot_general x8, matrix products, transform(): jnp.einsum('mjk,kl->mjl', left_i, cos_tab, precision=highest)  29.2 us
    dot_general x8, matrix products, transform(): jnp.einsum('jk,mkl->mjl', sin_tab, real_part, precision=highest)  25.5 us
    dot_general x8, matrix products, transform(): jnp.einsum('mjk,kl->mjl', left_r, sin_tab, precision=highest)  25.3 us
    dot_general x8, matrix products, transform(): jnp.einsum('mjk,kl->mjl', left_r, cos_tab, precision=highest)  22.6 us
  transfers between devices with their start and end apart: 4, of which 3 were waited for; matrix products, arithmetic and copies ran while one was open for 33% of the time, Pallas kernels for 0%

profile of v1, /device:TPU:1, one launch (start us, length us, event | category | flops | bytes accessed | tf_op | source)
XLA Modules:
  0.0 639.3 jit_solution(3221936872275931441)
XLA Ops:
  13.6 22.5 %collective-permute-done = f32[512,2,512]{2,1,0:T(2,128)} collective-permute-done((f32[512,2,512]{2,1,0:T(2,128)}, f32[512,2,512]{2,1,0:T(2,128)}, u32[]{:S(2)}, u32[]{:S(2)}) %collective-permute-start) | collective-permute-done | bytes 2097184 | tf_op jit(solution)/shard_map/ppermute | solution.py:13
  36.2 5.3 pad_maximum_fusion
  43.4 17.9 %while.35 = (s32[]{:T(128)}, f32[1024,2,512]{2,1,0:T(2,128)}, s32[4,3]{1,0:T(4,128)S(1)}, f32[4,256,2,256]{3,2,1,0:T(2,128)}, s32[]{:T(128)}) while((s32[]{:T(128)}, f32[1024,2,512]{2,1,0:T(2,128)}, s32[4,3]{1,0:T(4,128)S(1)}, f32[4,256,2,256]{3,2,1,0:T(2,128)}, s32[]{:T(128)}) %tuple.99), condition=%wide.while_cond, body=%wide.while_body.sunk | while | flops 2 | bytes 1050217 | solution.py:56
  44.0 3.8 bitcast_dynamic-update-slice_fusion.2
  48.5 3.8 bitcast_dynamic-update-slice_fusion.2
  53.0 3.8 bitcast_dynamic-update-slice_fusion.2
  57.4 3.8 bitcast_dynamic-update-slice_fusion.2
  63.1 249.8 %while.36 = (s32[]{:T(128)}, f32[4,256,2,256]{3,2,1,0:T(2,128)}, f32[4,2,256,256]{3,2,0,1:T(8,128)}, f32[256,256]{1,0:T(8,128)}, f32[4,256,2,256]{3,2,1,0:T(2,12...) while((s32[]{:T(128)}, f32[4,256,2,256]{3,2,1,0:T(2,128)}, ...), condition=%wide.region_4.5_spmd.clone.clone, body=%wide.region_0.4_spmd.clone.clone.sunk | while | flops 12915048448 | bytes 82838280 | solution.py:98
  90.8 3.6 fusion.231
  100.8 3.7 fusion.229
  105.1 4.6 fusion.232
  112.4 5.3 add_bitcast_fusion.2
  160.8 3.7 fusion.229
  165.2 4.8 fusion.232
  172.7 5.3 add_bitcast_fusion.2
  178.0 3.9 maximum_add_fusion.2
  222.7 3.7 fusion.229
  227.1 4.5 fusion.232
  234.3 5.3 add_bitcast_fusion.2
  239.6 3.9 maximum_add_fusion.2
  284.4 3.7 fusion.229
  288.7 4.6 fusion.232
  296.0 5.3 add_bitcast_fusion.2
  301.3 3.9 maximum_add_fusion.2
  319.1 209.0 %while.34 = (s32[]{:T(128)}, f32[1024,2,512]{2,1,0:T(2,128)}, s32[4]{0:T(128)S(1)}, s32[4]{0:T(128)S(1)}, f32[4,256,2,256]{3,2,1,0:T(2,128)}, /*index=5*/s32[]{:T(128)}, s32[]{:T(128)}, s32[]{:T(128)}, s32[]{:T(128)}) while((s32[]{:T(128)}, f32[1024,2,512]{2,1,0:T(2,128)}, s32[4]{0:T(128)S(1)}, s32[4]{0:T(128)S(1)}, ...), condition=%wide.region_6.7_spmd, body=%wide.region_5.6_spmd.sunk | while | flops 131080 | bytes 2621641 | solution.py:109
  326.4 45.0 %dynamic_update_slice.21 = f32[1024,2,512]{2,1,0:T(2,128)} dynamic-update-slice(f32[1024,2,512]{2,1,0:T(2,128)} %get-tuple-element.737, f32[256,2,256]{2,1,0:T(2,128)S(1)} %bitcast_add_fusion.2, s32[]{:T(128)S(6)} %select_n.175, s32[]{:T(128)} %constant.116.clone.1..sunk, s32[]{:T(128)S(6)} %select_n.176) | dynamic-update-slice | bytes 1048580 | tf_op jit(solution)/shard_map/while/body/eval_jaxpr/dynamic_update_slice | solution.py:105
  378.6 45.0 %dynamic_update_slice.21 = f32[1024,2,512]{2,1,0:T(2,128)} dynamic-update-slice(f32[1024,2,512]{2,1,0:T(2,128)} %get-tuple-element.737, f32[256,2,256]{2,1,0:T(2,128)S(1)} %bitcast_add_fusion.2, s32[]{:T(128)S(6)} %select_n.175, s32[]{:T(128)} %constant.116.clone.1..sunk, s32[]{:T(128)S(6)} %select_n.176) | dynamic-update-slice | bytes 1048580 | tf_op jit(solution)/shard_map/while/body/eval_jaxpr/dynamic_update_slice | solution.py:105
  430.9 45.0 %dynamic_update_slice.21 = f32[1024,2,512]{2,1,0:T(2,128)} dynamic-update-slice(f32[1024,2,512]{2,1,0:T(2,128)} %get-tuple-element.737, f32[256,2,256]{2,1,0:T(2,128)S(1)} %bitcast_add_fusion.2, s32[]{:T(128)S(6)} %select_n.175, s32[]{:T(128)} %constant.116.clone.1..sunk, s32[]{:T(128)S(6)} %select_n.176) | dynamic-update-slice | bytes 1048580 | tf_op jit(solution)/shard_map/while/body/eval_jaxpr/dynamic_update_slice | solution.py:105
  483.1 45.0 %dynamic_update_slice.21 = f32[1024,2,512]{2,1,0:T(2,128)} dynamic-update-slice(f32[1024,2,512]{2,1,0:T(2,128)} %get-tuple-element.737, f32[256,2,256]{2,1,0:T(2,128)S(1)} %bitcast_add_fusion.2, s32[]{:T(128)S(6)} %select_n.175, s32[]{:T(128)} %constant.116.clone.1..sunk, s32[]{:T(128)S(6)} %select_n.176) | dynamic-update-slice | bytes 1048580 | tf_op jit(solution)/shard_map/while/body/eval_jaxpr/dynamic_update_slice | solution.py:105
  534.7 22.4 %collective-permute-done.1 = f32[512,2,512]{2,1,0:T(2,128)} collective-permute-done((f32[512,2,512]{2,1,0:T(2,128)}, f32[512,2,512]{2,1,0:T(2,128)}, u32[]{:S(2)}, u32[]{:S(2)}) %collective-permute-start.1) | collective-permute-done | bytes 2097184 | tf_op jit(solution)/shard_map/ppermute | solution.py:13
  557.1 5.2 divide_subtract_fusion
  562.2 65.8 %all-reduce.7.cloned.1.call-done = (f32[4,2,256,256]{3,2,1,0:T(8,128)}, f32[256,256]{1,0:T(8,128)}) async-done(((f32[4,2,256,256]{3,2,1,0:T(8,128)}, f32[256,256]{1,0:T(8,128)}), (f32[4,2,256,256]{3,2,1,0:T(8,128)}, f32[256,256]{1,0:T(8,128)})) %all-reduce.7.cloned.1.call-update) | async-done | bytes 2359312 | tf_op jit(solution)/shard_map/psum | solution.py:99
  (166 shorter events, 213.9 us)
Async XLA Ops:
  7.2 526.6 %all-reduce.5.cloned.1.call-start = ((), (), s32[]{:S(2)}) async-start(), calls=%async_computation | async-start | bytes 4718592 | tf_op jit(solution)/shard_map/psum | solution.py:99
  7.2 29.0 %collective-permute-start = (f32[512,2,512]{2,1,0:T(2,128)}, f32[512,2,512]{2,1,0:T(2,128)}, u32[]{:S(2)}, u32[]{:S(2)}) collective-permute-start(f32[512,2,512]{2,1,0:T(2,128)} %param.9), channel_id=1, source_target_pairs={{8,0},{16,8},{24,16},{32,24},{40,32},{48,40},{56,48},{64,56},{72,6... | collective-permute-start | bytes 6291464 | tf_op jit(solution)/shard_map/ppermute | solution.py:13
  11.7 24.5 %copy-start.5 = (f32[512,2,512]{2,1,0:T(2,128)S(1)}, f32[512,2,512]{2,1,0:T(2,128)}, u32[]{:S(2)}) copy-start(f32[512,2,512]{2,1,0:T(2,128)} %param.9) | copy-start | bytes 6291460
  99.8 1.0 copy-start.1
  105.1 4.6 copy-start.2
  105.1 7.3 %copy-start = (f32[4,256,256]{1,2,0:T(8,128)S(1)}, f32[4,256,256]{1,2,0:T(8,128)}, u32[]{:S(2)}) copy-start(f32[4,256,256]{1,2,0:T(8,128)} %fusion.231) | copy-start | bytes 3145732 | tf_op jit(solution)/shard_map/while
  117.8 3.2 copy-start.3
  159.8 1.0 copy-start.1
  165.2 4.8 copy-start.2
  165.2 7.5 %copy-start = (f32[4,256,256]{1,2,0:T(8,128)S(1)}, f32[4,256,256]{1,2,0:T(8,128)}, u32[]{:S(2)}) copy-start(f32[4,256,256]{1,2,0:T(8,128)} %fusion.231) | copy-start | bytes 3145732 | tf_op jit(solution)/shard_map/while
  178.0 3.9 copy-start.3
  221.7 1.0 copy-start.1
  227.0 4.6 copy-start.2
  227.1 7.2 %copy-start = (f32[4,256,256]{1,2,0:T(8,128)S(1)}, f32[4,256,256]{1,2,0:T(8,128)}, u32[]{:S(2)}) copy-start(f32[4,256,256]{1,2,0:T(8,128)} %fusion.231) | copy-start | bytes 3145732 | tf_op jit(solution)/shard_map/while
  239.6 3.9 copy-start.3
  283.4 1.0 copy-start.1
  288.7 4.6 copy-start.2
  288.7 7.3 %copy-start = (f32[4,256,256]{1,2,0:T(8,128)S(1)}, f32[4,256,256]{1,2,0:T(8,128)}, u32[]{:S(2)}) copy-start(f32[4,256,256]{1,2,0:T(8,128)} %fusion.231) | copy-start | bytes 3145732 | tf_op jit(solution)/shard_map/while
  301.3 3.9 copy-start.3
  316.0 312.1 %all-reduce.7.cloned.1.call-start = ((), (), s32[]{:S(2)}) async-start(), calls=%async_computation.1 | async-start | bytes 4718592 | tf_op jit(solution)/shard_map/psum | solution.py:99
  531.7 2.1 copy-start.4
  531.7 25.3 %collective-permute-start.1 = (f32[512,2,512]{2,1,0:T(2,128)}, f32[512,2,512]{2,1,0:T(2,128)}, u32[]{:S(2)}, u32[]{:S(2)}) collective-permute-start(f32[512,2,512]{2,1,0:T(2,128)} %slice.43), channel_id=1, source_target_pairs={{0,8},{8,16},{16,24},{24,32},{32,40},{40,48},{48,56},{56,64},{64,7... | collective-permute-start | bytes 6291464 | tf_op jit(solution)/shard_map/ppermute | solution.py:13
Sparse Core Ops, SparseCore 0:
  316.1 129.3 all-reduce.4
  534.0 94.0 all-reduce.6
